TPU v7x, 32 devices: a whole 2x2x4 slice. The times are simulated.
32 devices in a mesh: groups: 2 (over x), seq: 16 (over z, y, core).
Axes of the slice: x: 2, y: 2, z: 4, core: 2. Of those that a mesh axis runs over, the one named last changes fastest.
Arguments:
- frames: bfloat16 [16384, 1024], P(('groups', 'seq')), parts along dimension 0, may hold values from -6 to 6
- context: bfloat16 [3072, 512], P(('groups', 'seq')), parts along dimension 0, may hold values from -6 to 6
- noise_level: int32 [128], P(('groups', 'seq')), parts along dimension 0, may hold values from 0 to 7
- alignment: int32 [128, 2], P(('groups', 'seq')), parts along dimension 0, may hold values from 0 to 31, as said below
- counts: int32 [128], P(('groups', 'seq')), parts along dimension 0, may hold values from 1 to 2
- band_width: int32 [16], replicated, may hold values from 0 to 2, as said below
- mod_table: float32 [8, 2048], replicated, may hold values from -3 to 3
- qkv_weight: bfloat16 [1024, 3072], replicated, may hold values from -0.1875 to 0.1875
- out_weight: bfloat16 [1024, 1024], replicated, may hold values from -0.1875 to 0.1875
- cross_query_weight: bfloat16 [1024, 512], replicated, may hold values from -0.1875 to 0.1875
- cross_kv_weight: bfloat16 [512, 1024], replicated, may hold values from -0.25 to 0.25
- cross_out_weight: bfloat16 [512, 1024], replicated, may hold values from -0.25 to 0.25
- banded_attender_factor: float32 [16], replicated, may hold values from 0.5 to 80
- cross_temp: float32 [8], replicated, may hold values from 0.5 to 80
Outputs:
- update: bfloat16 [16384, 1024], P(('groups', 'seq')), parts along dimension 0
There are 2 independent parts, one for each index of `groups`. A program takes and returns all parts, laid end to end along the dimension named above; an argument that names none is the same for every part. Nothing has to cross between parts.
Inputs may be any that keep to these rules, and one draw needn't show every extreme that they name: `alignment`: the entries of each list are distinct consecutive token blocks, all within 1 token blocks of (b * 2) // 4 for frame block b. Among the rows of one device, the list of the first frame block starts as low as that allows and the list of the last frame block ends as high as that allows and has all slots live, both within the excerpt's token blocks. `band_width`: some head has band width 2.
All inputs are finite; a program needn't handle non-finite values.
Results may differ from a plain program's by a relative error of at most 0.0045.
The roundings to bfloat16 on the way count: a program that leaves them out, or rounds other values in their place, can miss the bound.
Values may be sent and summed in bfloat16 or wider, within the bound.
A program may use at most 192 MiB of HBM per device.

v0:
```python
import jax
import jax.numpy as jnp
from jax import lax
from jax.sharding import PartitionSpec as P

BANDED_ATTEND_CT = 16
MIXED_ATTEND_CNT = 8
HD = 64
LEVELS = 8
BLK = 128
WMAX = 2
TOKB = 48
RCH = 1
ALIST = 2


def with_halo(block, sides, width):
    for axis, dim in sides:
        count = lax.axis_size(axis)
        forward = [(i, i + 1) for i in range(count - 1)]
        backward = [(target, source) for source, target in forward]
        low = lax.ppermute(
            lax.slice_in_dim(block, block.shape[dim] - width, None, axis=dim), axis, forward
        )
        high = lax.ppermute(lax.slice_in_dim(block, 0, width, axis=dim), axis, backward)
        block = jnp.concatenate([low, block, high], axis=dim)
    return block


def head_norm(matrix, heads):
    count_rows = matrix.shape[0]
    parts = matrix.reshape(count_rows, heads, -1)
    parts = parts * lax.rsqrt(jnp.mean(parts * parts, axis=-1, keepdims=True) + 1e-06)
    return parts.reshape(count_rows, -1)


def masked_softmax(scores, allowed):
    scores = jnp.where(allowed, scores, -jnp.inf)
    peak = jnp.max(scores, axis=-1, keepdims=True)
    powers = jnp.exp(scores - peak)
    return powers / jnp.sum(powers, axis=-1, keepdims=True)


def shards(
    frames,
    context,
    noise_level,
    alignment,
    counts,
    band_width,
    mod_table,
    qkv_weight,
    out_weight,
    cross_query_weight,
    cross_kv_weight,
    cross_out_weight,
    banded_attender_factor,
    cross_temp,
):
    frame_rows, model_width = frames.shape
    query_width = qkv_weight.shape[1] // 3
    cross_width = cross_query_weight.shape[1]
    devices = lax.axis_size("seq")
    device = lax.axis_index("seq")
    local_blocks = frame_rows // BLK
    total_blocks = local_blocks * devices
    input_arrays = frames.astype(jnp.float32)
    normed = input_arrays * lax.rsqrt(
        jnp.mean(input_arrays * input_arrays, axis=1, keepdims=True) + 1e-06
    )
    onehot = (noise_level[:, None] == jnp.arange(LEVELS, dtype=jnp.int32)[None, :]).astype(
        jnp.float32
    )
    modulation = jnp.dot(onehot, mod_table, precision=lax.Precision.HIGHEST)
    hidden = (
        (
            normed.reshape(local_blocks, BLK, model_width)
            * (1.0 + modulation[:, None, :model_width])
            + modulation[:, None, model_width:]
        )
        .reshape(frame_rows, model_width)
        .astype(jnp.bfloat16)
    )
    alignment_slack = WMAX * BLK
    projected = jnp.dot(hidden, qkv_weight, preferred_element_type=jnp.float32)
    queries = head_norm(projected[:, :query_width], BANDED_ATTEND_CT).astype(jnp.bfloat16)
    local_pairs = jnp.concatenate(
        [
            head_norm(projected[:, query_width : 2 * query_width], BANDED_ATTEND_CT).astype(
                jnp.bfloat16
            ),
            projected[:, 2 * query_width :].astype(jnp.bfloat16),
        ],
        1,
    )
    key_pairs = with_halo(local_pairs, (("seq", 0),), alignment_slack)
    token_rows_local = context.shape[0]
    token_blocks = token_rows_local // TOKB
    cross_margin = RCH * TOKB
    context_pad = with_halo(context, (("seq", 0),), cross_margin)
    cross_proj = jnp.dot(context_pad, cross_kv_weight, preferred_element_type=jnp.float32)
    cross_pairs = jnp.concatenate(
        [
            head_norm(cross_proj[:, :cross_width], MIXED_ATTEND_CNT).astype(jnp.bfloat16),
            cross_proj[:, cross_width:].astype(jnp.bfloat16),
        ],
        1,
    )
    window_tokens = cross_pairs.shape[0]
    cross_keys = cross_pairs[:, :cross_width].reshape(window_tokens, MIXED_ATTEND_CNT, HD)
    cross_values = cross_pairs[:, cross_width:].reshape(window_tokens, MIXED_ATTEND_CNT, HD)
    token_block = device * token_blocks - RCH + jnp.arange(window_tokens, dtype=jnp.int32) // TOKB
    live_slots = jnp.arange(ALIST, dtype=jnp.int32)[None, :] < counts[:, None]
    block_allowed = jnp.any(
        (alignment[:, :, None] == token_block[None, None, :]) & live_slots[:, :, None], axis=1
    )
    cross_queries = head_norm(
        jnp.dot(hidden, cross_query_weight, preferred_element_type=jnp.float32), MIXED_ATTEND_CNT
    ).astype(jnp.bfloat16)
    self_scale = banded_attender_factor * HD ** (-0.5)
    cross_scale = cross_temp * HD ** (-0.5)
    group_rows = min(frame_rows, 512)
    group_count = frame_rows // group_rows
    group_blocks = group_rows // BLK

    def attend(group):
        first_row = group * group_rows
        query_rows = queries.reshape(group_rows, BANDED_ATTEND_CT, HD)
        key_rows = key_pairs[:, :query_width].reshape(-1, BANDED_ATTEND_CT, HD)
        value_rows = key_pairs[:, query_width:].reshape(-1, BANDED_ATTEND_CT, HD)
        query_block = (
            device * local_blocks + (first_row + jnp.arange(group_rows, dtype=jnp.int32)) // BLK
        )
        key_block = (
            device * local_blocks
            - WMAX
            + (first_row + jnp.arange(group_rows + 2 * alignment_slack, dtype=jnp.int32)) // BLK
        )
        within_band_flag = (
            jnp.abs(query_block[:, None] - key_block[None, :])[None, :, :]
            <= band_width[:, None, None]
        ) & ((key_block >= 0) & (key_block < total_blocks))[None, None, :]
        scores = (
            jnp.einsum("ihd,jhd->hij", query_rows, key_rows, preferred_element_type=jnp.float32)
            * self_scale[:, None, None]
        )
        weights = masked_softmax(scores, within_band_flag).astype(jnp.bfloat16)
        self_out = (
            jnp.einsum("hij,jhd->ihd", weights, value_rows, preferred_element_type=jnp.float32)
            .reshape(group_rows, query_width)
            .astype(jnp.bfloat16)
        )
        cross_rows = cross_queries.reshape(group_rows, MIXED_ATTEND_CNT, HD)
        row_allowed = jnp.broadcast_to(
            block_allowed[:, None, :], (group_blocks, BLK, window_tokens)
        ).reshape(group_rows, window_tokens)
        cross_scores = (
            jnp.einsum("ihd,jhd->hij", cross_rows, cross_keys, preferred_element_type=jnp.float32)
            * cross_scale[:, None, None]
        )
        cross_weights = masked_softmax(cross_scores, row_allowed[None, :, :]).astype(jnp.bfloat16)
        cross_out = (
            jnp.einsum(
                "hij,jhd->ihd", cross_weights, cross_values, preferred_element_type=jnp.float32
            )
            .reshape(group_rows, cross_width)
            .astype(jnp.bfloat16)
        )
        total = jnp.dot(self_out, out_weight, preferred_element_type=jnp.float32) + jnp.dot(
            cross_out, cross_out_weight, preferred_element_type=jnp.float32
        )
        return total.astype(jnp.bfloat16)

    result = lax.map(attend, jnp.arange(group_count, dtype=jnp.int32))
    return result.reshape(frame_rows, model_width)


def solution(mesh):
    placed = (
        P(("groups", "seq"), None),
        P(("groups", "seq"), None),
        P(("groups", "seq")),
        P(("groups", "seq"), None),
        P(("groups", "seq")),
        P(),
        P(),
        P(),
        P(),
        P(),
        P(),
        P(),
        P(),
        P(),
    )
    return jax.shard_map(
        shards, mesh=mesh, in_specs=placed, out_specs=P(("groups", "seq"), None), check_vma=False
    )
```

profile of v0, /device:TPU:25, one launch (start us, length us, event | category | flops | bytes accessed | tf_op | source)
XLA Modules:
  0.0 131.6 jit_solution(831613482611971934)
XLA Ops:
  1.0 3.8 %collective-permute-start.2 = (bf16[48,512]{1,0:T(8,128)(2,1)S(1)}, bf16[48,512]{1,0:T(8,128)(2,1)S(1)}, u32[]{:S(2)}, u32[]{:S(2)}) collective-permute-start(bf16[48,512]{1,0:T(8,128)(2,1)S(1)} %get-tuple-element.39), channel_id=1, source_target_pairs={{0,1},{1,2},{2,3},{3,4},{4,5},{5,6},{6,7},{7,8},{8,9},{9,10},{10,1... | collective-permute-start | bytes 147464 | tf_op jit(solution)/shard_map/ppermute | solution.py:22
  4.8 1.9 %collective-permute-start.3 = (bf16[48,512]{1,0:T(8,128)(2,1)S(1)}, bf16[48,512]{1,0:T(8,128)(2,1)S(1)}, u32[]{:S(2)}, u32[]{:S(2)}) collective-permute-start(bf16[48,512]{1,0:T(8,128)(2,1)S(1)} %get-tuple-element.40), channel_id=1, source_target_pairs={{1,0},{2,1},{3,2},{4,3},{5,4},{6,5},{7,6},{8,7},{9,8},{10,9},{11,1... | collective-permute-start | bytes 147464 | tf_op jit(solution)/shard_map/ppermute | solution.py:25
  9.8 5.9 %fusion.51 = f32[512,3072]{1,0:T(8,128)S(1)} fusion(bf16[512,1024]{1,0:T(8,128)(2,1)S(1)} %fusion.13, bf16[1024,3072]{1,0:T(8,128)(2,1)} %param.21), kind=kOutput, calls=%fused_computation.102 | convolution fusion | flops 3221225472 | bytes 13631488 | tf_op jit(solution)/shard_map/dot_general | solution.py:85
  17.1 2.9 %slice_multiply_fusion = (f32[512,1024]{1,0:T(8,128)}, f32[512,1024]{1,0:T(8,128)}) fusion(f32[512,3072]{1,0:T(8,128)S(1)} %fusion.51), kind=kLoop, calls=%fused_computation.32 | loop fusion | flops 1048576 | bytes 8388608 | tf_op jit(solution)/shard_map/mul | solution.py:33
  20.0 2.9 %copy.38 = f32[512,1024]{0,1:T(8,128)} copy(f32[512,1024]{1,0:T(8,128)} %get-tuple-element.33) | data formatting | bytes 4194304 | tf_op jit(solution)/shard_map/mul | solution.py:33
  22.9 1.9 %bitcast_reduce_fusion = f32[512,16]{0,1:T(8,128)S(1)} fusion(f32[512,1024]{0,1:T(8,128)} %copy.38), kind=kLoop, calls=%fused_computation.26 | loop fusion | flops 516096 | bytes 2129920 | tf_op jit(solution)/shard_map/reduce_sum | solution.py:33
  26.3 2.9 %copy.39 = f32[512,1024]{1,0:T(8,128)} copy(f32[512,1024]{0,1:T(8,128)} %bitcast.54) | data formatting | bytes 4194304 | tf_op jit(solution)/shard_map/mul | solution.py:33
  29.2 2.9 %copy.35 = f32[512,1024]{0,1:T(8,128)} copy(f32[512,1024]{1,0:T(8,128)} %get-tuple-element.34) | data formatting | bytes 4194304 | tf_op jit(solution)/shard_map/mul | solution.py:33
  32.1 1.9 %bitcast_reduce_fusion.1 = f32[512,16]{0,1:T(8,128)S(1)} fusion(f32[512,1024]{0,1:T(8,128)} %copy.35), kind=kLoop, calls=%fused_computation.27 | loop fusion | flops 516096 | bytes 2129920 | tf_op jit(solution)/shard_map/reduce_sum | solution.py:33
  35.6 2.9 %copy.36 = f32[512,1024]{1,0:T(8,128)} copy(f32[512,1024]{0,1:T(8,128)} %bitcast.55) | data formatting | bytes 4194304 | tf_op jit(solution)/shard_map/mul | solution.py:33
  38.5 5.2 %multiply_convert_fusion = (bf16[512,1024]{1,0:T(8,128)(2,1)}, bf16[512,1024]{1,0:T(8,128)(2,1)S(1)}) fusion(f32[512,1024]{1,0:T(8,128)} %copy.39, f32[512,3072]{1,0:T(8,128)} %copy-done.1, f32[512,1024]{1,0:T(8,128)} %copy.36), kind=kLoop, calls=%fused_computation.29 | loop fusion | flops 2097152 | bytes 10485760 | tf_op jit(solution)/shard_map/convert_element_type | solution.py:86
  45.3 3.6 %collective-permute-start = (bf16[256,2048]{1,0:T(8,128)(2,1)}, bf16[256,2048]{1,0:T(8,128)(2,1)}, u32[]{:S(2)}, u32[]{:S(2)}) collective-permute-start(bf16[256,2048]{1,0:T(8,128)(2,1)} %get-tuple-element.37), channel_id=1, source_target_pairs={{0,1},{1,2},{2,3},{3,4},{4,5},{5,6},{6,7},{7,8},{8,9},{9,10},{10,1... | collective-permute-start | bytes 3145736 | tf_op jit(solution)/shard_map/ppermute | solution.py:22
  48.9 2.1 %collective-permute-start.1 = (bf16[256,2048]{1,0:T(8,128)(2,1)}, bf16[256,2048]{1,0:T(8,128)(2,1)}, u32[]{:S(2)}, u32[]{:S(2)}) collective-permute-start(bf16[256,2048]{1,0:T(8,128)(2,1)} %get-tuple-element.38), channel_id=1, source_target_pairs={{1,0},{2,1},{3,2},{4,3},{5,4},{6,5},{7,6},{8,7},{9,8},{10,9},{11,1... | collective-permute-start | bytes 3145736 | tf_op jit(solution)/shard_map/ppermute | solution.py:25
  52.2 2.3 %copy.44 = bf16[1024,512]{0,1:T(8,128)(2,1)} copy(bf16[1024,512]{1,0:T(8,128)(2,1)} %param.23) | data formatting | bytes 2097152 | tf_op args[9]
  54.5 3.3 %multiply_reduce_fusion = (f32[512,8]{0,1:T(8,128)S(1)}, f32[512,8,64]{0,2,1:T(8,128)}) fusion(bf16[8,64,1024]{2,1,0:T(8,128)(2,1)} %bitcast.62, bf16[512,1024]{1,0:T(8,128)(2,1)} %copy-done.6), kind=kOutput, calls=%fused_computation.45 | convolution fusion | flops 537391104 | bytes 3162112 | tf_op jit(solution)/shard_map/dot_general | solution.py:118
  61.3 2.3 %copy.40 = bf16[512,1024]{0,1:T(8,128)(2,1)} copy(bf16[512,1024]{1,0:T(8,128)(2,1)} %get-tuple-element.31) | data formatting | bytes 2097152 | tf_op jit(solution)/shard_map/convert_element_type | solution.py:86
  66.2 1.8 %copy.42 = bf16[192,512]{0,1:T(8,128)(2,1)} copy(bf16[192,512]{1,0:T(8,128)(2,1)} %slice.83) | data formatting | bytes 393216 | tf_op jit(solution)/shard_map/slice | solution.py:105
  75.0 1.9 %fusion.23 = f32[8,512,192]{1,2,0:T(8,128)S(1)} fusion(bf16[192,8,64]{0,2,1:T(8,128)(2,1)S(1)} %bitcast.60, f32[512,8,64]{0,2,1:T(8,128)} %get-tuple-element.62, f32[512,8]{0,1:T(8,128)S(1)} %add_rsqrt_fusion.2), kind=kOutput, calls=%fused_computation.46 | convolution fusion | flops 101187584 | bytes 4407296 | tf_op jit(solution)/shard_map/while/body/eval_jaxpr/ihd,jhd->hij/dot_general | solution.py:158
  79.6 2.7 %pad_maximum_fusion = bf16[1024,2048]{1,0:T(8,128)(2,1)S(1)} fusion(bf16[256,2048]{1,0:T(8,128)(2,1)} %collective-permute-done.1, bf16[512,1024]{1,0:T(8,128)(2,1)S(1)} %copy-done.3, bf16[512,1024]{1,0:T(8,128)(2,1)S(1)} %get-tuple-element.32, bf16[256,2048]{1,0:T(8,128)(2,1)} %collective-permute-done), kind=kLoop, calls=%fused_computation.12 | loop fusion | flops 16777216 | bytes 8388608 | tf_op jit(solution)/shard_map/concatenate | solution.py:26
  82.4 2.4 %fusion.45 = (bf16[1024,1024]{1,0:T(8,128)(2,1)}, bf16[1024,1024]{1,0:T(8,128)(2,1)}) fusion(bf16[1024,2048]{1,0:T(8,128)(2,1)S(1)} %pad_maximum_fusion), kind=kLoop, calls=%fused_computation.97 | loop fusion | bytes 8388608 | tf_op jit(solution)/shard_map/while/body/eval_jaxpr/slice | solution.py:129
  84.8 4.0 %copy.41 = bf16[1024,1024]{0,1:T(8,128)(2,1)} copy(bf16[1024,1024]{1,0:T(8,128)(2,1)} %get-tuple-element.35) | data formatting | bytes 4194304 | tf_op jit(solution)/shard_map/while/body/eval_jaxpr/slice | solution.py:129
  88.7 4.0 %copy.37 = bf16[1024,1024]{0,1:T(8,128)(2,1)} copy(bf16[1024,1024]{1,0:T(8,128)(2,1)} %get-tuple-element.36) | data formatting | bytes 4194304 | tf_op jit(solution)/shard_map/while/body/eval_jaxpr/slice | solution.py:130
  92.8 21.8 %fusion.47 = (f32[16,512]{1,0:T(8,128)S(1)}, f32[16,512,1024]{2,1,0:T(8,128)}) fusion(f32[16]{0:T(128)S(1)} %copy-done.19, s32[512,1024]{1,0:T(8,128)} %subtract_abs_fusion, s32[16]{0:T(128)S(1)} %copy-done.17, pred[1024]{0:T(1024)(128)(4,1)S(1)} %copy-done.18, bf16[512,16,64]{0,2,1:T(8,128)(2,1)S(1)} %bitcast.61, bf16[1024,16,64]{0,2,1:T(8,128)(2,1)} %bitcast.57), kind=kOutput, calls=%fused_computation.99 | convolution fusion | flops 1124074496 | bytes 38831232 | tf_op jit(solution)/shard_map/while/body/eval_jaxpr/sub | solution.py:40
  114.6 13.9 %fusion.18 = bf16[16,64,512]{2,1,0:T(8,128)(2,1)S(1)} fusion(bf16[1024,16,64]{0,2,1:T(8,128)(2,1)} %bitcast.58, f32[16,512,1024]{2,1,0:T(8,128)} %get-tuple-element.60, f32[16,512]{1,0:T(8,128)S(1)} %get-tuple-element.58), kind=kOutput, calls=%fused_computation.38 | convolution fusion | flops 1091043328 | bytes 36732928 | tf_op jit(solution)/shard_map/while/body/eval_jaxpr/hij,jhd->ihd/dot_general | solution.py:149
  (85 shorter events, 30.0 us)
Async XLA Ops:
  0.0 128.5 %copy-start = (bf16[1024,1024]{1,0:T(8,128)(2,1)S(1)}, bf16[1024,1024]{1,0:T(8,128)(2,1)}, u32[]{:S(2)}) copy-start(bf16[1024,1024]{1,0:T(8,128)(2,1)} %param.22) | copy-start | bytes 6291460
  0.0 9.4 %copy-start.4 = (bf16[512,1024]{1,0:T(8,128)(2,1)S(1)}, bf16[512,1024]{1,0:T(8,128)(2,1)}, u32[]{:S(2)}) copy-start(bf16[512,1024]{1,0:T(8,128)(2,1)} %param.14) | copy-start | bytes 3145732
  1.0 62.6 %collective-permute-start.2 = (bf16[48,512]{1,0:T(8,128)(2,1)S(1)}, bf16[48,512]{1,0:T(8,128)(2,1)S(1)}, u32[]{:S(2)}, u32[]{:S(2)}) collective-permute-start(bf16[48,512]{1,0:T(8,128)(2,1)S(1)} %get-tuple-element.39), channel_id=1, source_target_pairs={{0,1},{1,2},{2,3},{3,4},{4,5},{5,6},{6,7},{7,8},{8,9},{9,10},{10,1... | collective-permute-start | bytes 147464 | tf_op jit(solution)/shard_map/ppermute | solution.py:22
  4.8 58.8 %collective-permute-start.3 = (bf16[48,512]{1,0:T(8,128)(2,1)S(1)}, bf16[48,512]{1,0:T(8,128)(2,1)S(1)}, u32[]{:S(2)}, u32[]{:S(2)}) collective-permute-start(bf16[48,512]{1,0:T(8,128)(2,1)S(1)} %get-tuple-element.40), channel_id=1, source_target_pairs={{1,0},{2,1},{3,2},{4,3},{5,4},{6,5},{7,6},{8,7},{9,8},{10,9},{11,1... | collective-permute-start | bytes 147464 | tf_op jit(solution)/shard_map/ppermute | solution.py:25
  9.8 5.9 %copy-start.6 = (bf16[512,1024]{1,0:T(8,128)(2,1)}, bf16[512,1024]{1,0:T(8,128)(2,1)S(1)}, u32[]{:S(2)}) copy-start(bf16[512,1024]{1,0:T(8,128)(2,1)S(1)} %fusion.13) | copy-start | bytes 3145732
  15.7 4.3 %copy-start.1 = (f32[512,3072]{1,0:T(8,128)}, f32[512,3072]{1,0:T(8,128)S(1)}, u32[]{:S(2)}) copy-start(f32[512,3072]{1,0:T(8,128)S(1)} %fusion.51) | copy-start | bytes 18874372
  38.5 5.3 %copy-start.2 = (bf16[512,1024]{1,0:T(8,128)(2,1)S(1)}, bf16[512,1024]{1,0:T(8,128)(2,1)}, u32[]{:S(2)}) copy-start(bf16[512,1024]{1,0:T(8,128)(2,1)} %slice.82) | copy-start | bytes 3145732
  43.8 7.3 %copy-start.14 = (s32[4]{0:T(128)S(1)}, s32[4]{0:T(128)}, u32[]{:S(2)}) copy-start(s32[4]{0:T(128)} %param.18) | copy-start | bytes 52
  43.8 7.3 %copy-start.15 = (f32[16]{0:T(128)S(1)}, f32[16]{0:T(128)}, u32[]{:S(2)}) copy-start(f32[16]{0:T(128)} %param.26) | copy-start | bytes 196
  43.8 7.9 %copy-start.16 = (f32[8]{0:T(128)S(1)}, f32[8]{0:T(128)}, u32[]{:S(2)}) copy-start(f32[8]{0:T(128)} %param.27) | copy-start | bytes 100
  45.3 34.4 %collective-permute-start = (bf16[256,2048]{1,0:T(8,128)(2,1)}, bf16[256,2048]{1,0:T(8,128)(2,1)}, u32[]{:S(2)}, u32[]{:S(2)}) collective-permute-start(bf16[256,2048]{1,0:T(8,128)(2,1)} %get-tuple-element.37), channel_id=1, source_target_pairs={{0,1},{1,2},{2,3},{3,4},{4,5},{5,6},{6,7},{7,8},{8,9},{9,10},{10,1... | collective-permute-start | bytes 3145736 | tf_op jit(solution)/shard_map/ppermute | solution.py:22
  48.9 30.7 %collective-permute-start.1 = (bf16[256,2048]{1,0:T(8,128)(2,1)}, bf16[256,2048]{1,0:T(8,128)(2,1)}, u32[]{:S(2)}, u32[]{:S(2)}) collective-permute-start(bf16[256,2048]{1,0:T(8,128)(2,1)} %get-tuple-element.38), channel_id=1, source_target_pairs={{1,0},{2,1},{3,2},{4,3},{5,4},{6,5},{7,6},{8,7},{9,8},{10,9},{11,1... | collective-permute-start | bytes 3145736 | tf_op jit(solution)/shard_map/ppermute | solution.py:25
  57.8 1.7 %copy-start.13 = (s32[4,2]{0,1:T(2,128)S(1)}, s32[4,2]{0,1:T(2,128)}, u32[]{:S(2)}) copy-start(s32[4,2]{0,1:T(2,128)} %param.17) | copy-start | bytes 100
  57.8 5.8 %copy-start.10 = (bf16[96,512]{1,0:T(8,128)(2,1)S(1)}, bf16[96,512]{1,0:T(8,128)(2,1)}, u32[]{:S(2)}) copy-start(bf16[96,512]{1,0:T(8,128)(2,1)} %param.15) | copy-start | bytes 294916
  75.0 1.9 %copy-start.12 = (pred[24,8,4,128]{3,1,2,0:T(8,128)(4,1)S(1)}, pred[24,8,4,128]{3,1,2,0:T(8,128)(4,1)}, u32[]{:S(2)}) copy-start(pred[24,8,4,128]{3,1,2,0:T(8,128)(4,1)} %copy.50) | copy-start | bytes 294916
  75.0 1.9 %copy-start.20 = (f32[8]{0:T(128)S(1)}, f32[8]{0:T(128)}, u32[]{:S(2)}) copy-start(f32[8]{0:T(128)} %broadcast_multiply_fusion) | copy-start | bytes 100
  76.9 1.5 %copy-start.11 = (bf16[192,512]{0,1:T(8,128)(2,1)S(1)}, bf16[192,512]{0,1:T(8,128)(2,1)}, u32[]{:S(2)}) copy-start(bf16[192,512]{0,1:T(8,128)(2,1)} %copy.42) | copy-start | bytes 589828
  78.4 1.3 copy-start.3
  88.7 4.0 %copy-start.7 = (bf16[512,1024]{0,1:T(8,128)(2,1)S(1)}, bf16[512,1024]{0,1:T(8,128)(2,1)}, u32[]{:S(2)}) copy-start(bf16[512,1024]{0,1:T(8,128)(2,1)} %copy.40) | copy-start | bytes 3145732
  88.7 4.0 %copy-start.17 = (s32[16]{0:T(128)S(1)}, s32[16]{0:T(128)}, u32[]{:S(2)}) copy-start(s32[16]{0:T(128)} %param.19) | copy-start | bytes 196
  88.7 4.0 %copy-start.18 = (pred[1024]{0:T(1024)(128)(4,1)S(1)}, pred[1024]{0:T(1024)(128)(4,1)}, u32[]{:S(2)}) copy-start(pred[1024]{0:T(1024)(128)(4,1)} %compare_and_fusion) | copy-start | bytes 3076
  88.7 4.0 %copy-start.19 = (f32[16]{0:T(128)S(1)}, f32[16]{0:T(128)}, u32[]{:S(2)}) copy-start(f32[16]{0:T(128)} %broadcast_multiply_fusion.1) | copy-start | bytes 196
  128.5 1.3 copy-start.8
  128.5 1.3 %copy-start.9 = (bf16[8,64,512]{2,1,0:T(8,128)(2,1)S(1)}, bf16[8,64,512]{2,1,0:T(8,128)(2,1)}, u32[]{:S(2)}) copy-start(bf16[8,64,512]{2,1,0:T(8,128)(2,1)} %fusion.19) | copy-start | bytes 1572868
  (1 other events, 0.9 us)
where the time goes:
time: 134 us; the launch traced here: 132 us
  matrix products  53.7 us (40%)
  local copies, waits for them, and re-layouts  40.2 us (30%)
  other arithmetic  25.8 us (19%)
  starting transfers between devices  11.5 us (9%)
    sub x1, matrix products, masked_softmax(): powers = jnp.exp(scores - peak)  21.8 us
    dot_general x1, matrix products, attend(): jnp.einsum('hij,jhd->ihd', weights, value_rows, preferred_element_type=jn...  13.9 us
    mul x6, local copies, waits for them, and re-layouts, head_norm(): parts * lax.rsqrt(jnp.mean(parts * parts, axis=-1, keepdims=True) + 1e-06)  11 us
    ppermute x2, starting transfers between devices, with_halo(): lax.ppermute(lax.slice_in_dim(block, block.shape[dim] - width, None, axis...  7.46 us
    mul x3, local copies, waits for them, and re-layouts, head_norm(): parts * parts  6.79 us
    slice x2, local copies, waits for them, and re-layouts, attend(): key_rows = key_pairs[:, :query_width].reshape(-1, BANDED_ATTEND_CT, HD)  6.37 us
    dot_general x1, matrix products, shards(): projected = jnp.dot(hidden, qkv_weight, preferred_element_type=jnp.float32)  5.9 us
    convert_element_type x1, other arithmetic, shards(): head_norm(projected[:, :query_width], BANDED_ATTEND_CT).astype(jnp.bfloat16)  5.25 us
  transfers between devices with their start and end apart: 4, of which 0 were waited for; matrix products, arithmetic and copies ran while one was open for 51% of the time, Pallas kernels for 0%

commit v1 on v0

v1 whole, which is shorter than its diff:
```python
import functools
import math

import jax
import jax.numpy as jnp
from jax import lax
from jax.experimental import pallas as pl
from jax.experimental.pallas import tpu as pltpu
from jax.sharding import PartitionSpec as P

BANDED_ATTEND_CT = 16
MIXED_ATTEND_CNT = 8
HD = 64
LEVELS = 8
BLK = 128
WMAX = 2
TOKB = 48
RCH = 1
ALIST = 2
PAIR = 2 * HD
HALO = WMAX * BLK
CHUNK = 256
EPS = 1e-06
SAFE_FACTOR = 6.0
MESH = pl.DeviceIdType.MESH


def pair_norm(part):
    low = lax.broadcasted_iota(jnp.int32, part.shape, 1) < HD
    square = part * part
    first = jnp.sum(jnp.where(low, square, 0.0), axis=-1, keepdims=True)
    second = jnp.sum(jnp.where(low, 0.0, square), axis=-1, keepdims=True)
    mean = jnp.where(low, first, second) * (1.0 / HD)
    return part * lax.rsqrt(mean + EPS)


def project_kernel(
    devices,
    frames,
    context,
    noise,
    mod,
    wqkv,
    wcq,
    wckv,
    q_out,
    k_out,
    v_out,
    cq_out,
    ck_out,
    cv_out,
    window,
    tokens,
    noise_halo,
    hidden,
    wqkv_v,
    wcq_v,
    wckv_v,
    local_sem,
    weight_sem,
    send_sem,
    recv_sem,
):
    me = lax.axis_index("seq")
    rows, width = frames.shape
    blocks = rows // BLK
    token_rows = context.shape[0]
    margin = RCH * TOKB
    qw = q_out.shape[1]
    cw = cq_out.shape[1]
    has = (me > 0, me < devices - 1)

    fetch_frames = pltpu.make_async_copy(
        frames, window.at[pl.ds(HALO, rows), :], local_sem.at[0]
    )
    fetch_tokens = pltpu.make_async_copy(
        context, tokens.at[pl.ds(margin, token_rows), :], local_sem.at[1]
    )
    fetch_frames.start()
    weight_order = (1, 2, 0)
    fetch_w = {}
    for slot in weight_order:
        cols = pl.ds(slot * qw, qw)
        fetch_w[slot] = pltpu.make_async_copy(
            wqkv.at[:, cols], wqkv_v.at[:, cols], weight_sem.at[slot]
        )
        fetch_w[slot].start()
    fetch_cq = pltpu.make_async_copy(wcq, wcq_v, weight_sem.at[3])
    fetch_ckv = pltpu.make_async_copy(wckv, wckv_v, weight_sem.at[4])

    barrier = pltpu.get_barrier_semaphore()
    for side in (0, 1):

        @pl.when(has[side])
        def _(side=side):
            pl.semaphore_signal(
                barrier, inc=1, device_id={"seq": me + 2 * side - 1}, device_id_type=MESH
            )

    peers = jnp.minimum(me, 1) + jnp.minimum(devices - 1 - me, 1)
    pl.semaphore_wait(barrier, peers)

    def copies(side):
        other = 1 - side
        peer = {"seq": me + 2 * side - 1}
        edge = rows - HALO if side else 0
        land = 0 if side else HALO + rows
        token_edge = token_rows - margin if side else 0
        token_land = 0 if side else margin + token_rows
        triples = (
            (noise, noise_halo.at[other]),
            (frames.at[pl.ds(edge, HALO), :], window.at[pl.ds(land, HALO), :]),
            (
                context.at[pl.ds(token_edge, margin), :],
                tokens.at[pl.ds(token_land, margin), :],
            ),
        )
        return [
            pltpu.make_async_remote_copy(
                src_ref=source,
                dst_ref=target,
                send_sem=send_sem.at[side, index],
                recv_sem=recv_sem.at[other, index],
                device_id=peer,
                device_id_type=MESH,
            )
            for index, (source, target) in enumerate(triples)
        ]

    sends = [copies(0), copies(1)]
    for side in (0, 1):

        @pl.when(has[side])
        def _(side=side):
            for copy in sends[side]:
                copy.start()

    fetch_cq.start()
    fetch_ckv.start()
    fetch_tokens.start()

    def make_hidden(row, level):
        scale = jnp.zeros((1, width), jnp.float32)
        shift = jnp.zeros((1, width), jnp.float32)
        for entry in range(LEVELS):
            here = level == entry
            scale = jnp.where(here, mod[entry : entry + 1, :width], scale)
            shift = jnp.where(here, mod[entry : entry + 1, width:], shift)
        place = pl.ds(pl.multiple_of(row, BLK), BLK)
        values = window[place, :].astype(jnp.float32)
        mean = jnp.mean(values * values, axis=1, keepdims=True)
        normed = values * lax.rsqrt(mean + EPS)
        hidden[place, :] = (normed * (1.0 + scale) + shift).astype(jnp.bfloat16)

    def project(source, place, weight, first_col, target, normalize):
        total = target.shape[1]

        def step(index, carry):
            out_cols = pl.multiple_of(index * CHUNK, CHUNK)
            y = jnp.dot(
                source[place, :],
                weight[:, pl.ds(pl.multiple_of(first_col + index * CHUNK, CHUNK), CHUNK)],
                preferred_element_type=jnp.float32,
            )
            for part in range(CHUNK // PAIR):
                piece = y[:, part * PAIR : (part + 1) * PAIR]
                if normalize:
                    piece = pair_norm(piece)
                target[place_of(target, place), pl.ds(out_cols + part * PAIR, PAIR)] = (
                    piece.astype(jnp.bfloat16)
                )
            return carry

        lax.fori_loop(0, total // CHUNK, step, 0)

    def place_of(target, place):
        if target.shape[0] == rows:
            return pl.ds(0, rows)
        return place

    fetch_frames.wait()
    for block in range(blocks):
        make_hidden(HALO + block * BLK, noise[:, block : block + 1])
    local = pl.ds(HALO, rows)
    fetch_w[1].wait()
    project(hidden, local, wqkv_v, qw, k_out, True)
    fetch_w[2].wait()
    project(hidden, local, wqkv_v, 2 * qw, v_out, False)
    fetch_w[0].wait()
    project(hidden, local, wqkv_v, 0, q_out, True)
    fetch_cq.wait()
    project(hidden, local, wcq_v, 0, cq_out, True)

    fetch_ckv.wait()
    fetch_tokens.wait()

    def halo_step(step, carry):
        side = lax.rem(me + 1 + step, 2)
        present = jnp.where(side == 0, me > 0, me < devices - 1)
        row = pl.multiple_of(side * (HALO + rows), BLK)
        token_row = pl.multiple_of(side * (margin + token_rows), 16)

        @pl.when(present)
        def _():
            waits = (
                noise_halo.at[0],
                window.at[pl.ds(0, HALO), :],
                tokens.at[pl.ds(0, margin), :],
            )
            for index, ref in enumerate(waits):
                pltpu.make_async_copy(ref, ref, recv_sem.at[side, index]).wait()
            levels = noise_halo[side]
            for block in range(WMAX):
                low_side = levels[:, blocks - WMAX + block : blocks - WMAX + block + 1]
                level = jnp.where(side == 0, low_side, levels[:, block : block + 1])
                make_hidden(row + block * BLK, level)

        @pl.when(jnp.logical_not(present))
        def _():
            hidden[pl.ds(row, HALO), :] = jnp.zeros((HALO, width), jnp.bfloat16)
            tokens[pl.ds(token_row, margin), :] = jnp.zeros(
                (margin, tokens.shape[1]), jnp.bfloat16
            )

        place = pl.ds(row, HALO)
        project(hidden, place, wqkv_v, qw, k_out, True)
        project(hidden, place, wqkv_v, 2 * qw, v_out, False)
        return carry

    lax.fori_loop(0, 2, halo_step, 0)
    every = pl.ds(0, tokens.shape[0])
    project(tokens, every, wckv_v, 0, ck_out, True)
    project(tokens, every, wckv_v, cw, cv_out, False)

    for side in (0, 1):

        @pl.when(has[side])
        def _(side=side):
            for copy in sends[side]:
                copy.wait_send()


def attend_kernel(
    devices,
    me_ref,
    band,
    factor,
    temp,
    alignment,
    counts,
    q,
    k,
    v,
    cq,
    ck,
    cv,
    wo,
    wco,
    out,
    values,
    acc,
    self_out,
    cross_out,
    wo_v,
    wco_v,
    sem,
):
    me = me_ref[0]
    rows = q.shape[0]
    blocks = rows // BLK
    window_rows = k.shape[0]
    span = ALIST * TOKB
    fetch_wo = pltpu.make_async_copy(wo, wo_v, sem.at[0])
    fetch_wco = pltpu.make_async_copy(wco, wco_v, sem.at[1])
    fetch_wo.start()
    fetch_wco.start()
    to_base2 = HD ** (-0.5) * math.log2(math.e)

    def half(shape, parity):
        lane = lax.broadcasted_iota(jnp.int32, shape, 1)
        return (lane < HD) if parity == 0 else (lane >= HD)

    def scores_of(query, key):
        return lax.dot_general(
            query, key, (((1,), (1,)), ((), ())), preferred_element_type=jnp.float32
        )

    def shifted_powers(scores, allowed):
        scores = jnp.where(allowed, scores, -jnp.inf)
        return jnp.exp2(scores - jnp.max(scores, axis=-1, keepdims=True))

    def combine(target, cols):
        for block in range(blocks):
            place = pl.ds(block * BLK, BLK)
            first = acc[0, place, :]
            second = acc[1, place, :]
            low = half(first.shape, 0)
            total = pltpu.roll(jnp.where(low, second, first), HD, 1)
            target[place, cols] = (jnp.where(low, first, second) / total).astype(jnp.bfloat16)

    def self_pair(pair, carry):
        cols = pl.ds(pl.multiple_of(pair * PAIR, PAIR), PAIR)
        for parity in (0, 1):
            head = 2 * pair + parity
            reach = band[head]
            scale = factor[head] * to_base2
            safe = factor[head] <= SAFE_FACTOR
            row_block = (
                lax.broadcasted_iota(jnp.int32, (window_rows, PAIR), 0) // BLK
                + me * blocks
                - WMAX
            )
            valid = (row_block >= 0) & (row_block < devices * blocks)
            ones = jnp.where(valid, 1.0, 0.0).astype(jnp.bfloat16)
            values[parity] = jnp.where(half((window_rows, PAIR), parity), v[:, cols], ones)
            for size in range(WMAX + 1):

                @pl.when(safe & (reach == size))
                def _(size=size, parity=parity):
                    for block in range(blocks):
                        query = q[pl.ds(block * BLK, BLK), cols]
                        query = jnp.where(half(query.shape, parity), query, jnp.zeros_like(query))
                        keys = pl.ds((block + WMAX - size) * BLK, (2 * size + 1) * BLK)
                        powers = jnp.exp2(scores_of(query, k[keys, cols]) * scale)
                        acc[parity, pl.ds(block * BLK, BLK), :] = jnp.dot(
                            powers.astype(jnp.bfloat16),
                            values[parity, keys, :],
                            preferred_element_type=jnp.float32,
                        )

            @pl.when(jnp.logical_not(safe))
            def _(parity=parity):
                def one(block, inner):
                    first = pl.multiple_of(block * BLK, BLK)
                    query = q[pl.ds(first, BLK), cols]
                    query = jnp.where(half(query.shape, parity), query, jnp.zeros_like(query))
                    keys = pl.ds(first, (2 * WMAX + 1) * BLK)
                    scores = scores_of(query, k[keys, cols]) * scale
                    offset = lax.broadcasted_iota(jnp.int32, scores.shape, 1) // BLK - WMAX
                    key_block = offset + block + me * blocks
                    allowed = (
                        (jnp.abs(offset) <= reach)
                        & (key_block >= 0)
                        & (key_block < devices * blocks)
                    )
                    acc[parity, pl.ds(first, BLK), :] = jnp.dot(
                        shifted_powers(scores, allowed).astype(jnp.bfloat16),
                        values[parity, keys, :],
                        preferred_element_type=jnp.float32,
                    )
                    return inner

                lax.fori_loop(0, blocks, one, 0)

        combine(self_out, cols)
        return carry

    lax.fori_loop(0, BANDED_ATTEND_CT // 2, self_pair, 0)

    token_blocks = ck.shape[0] // TOKB - 2 * RCH

    def cross_pair(pair, carry):
        cols = pl.ds(pl.multiple_of(pair * PAIR, PAIR), PAIR)
        for parity in (0, 1):
            head = 2 * pair + parity
            scale = temp[head] * to_base2
            safe = temp[head] <= SAFE_FACTOR

            def run(shifted, parity=parity, scale=scale):
                for block in range(blocks):
                    lowest = jnp.minimum(alignment[block, 0], alignment[block, 1])
                    live = counts[block]
                    admit = [
                        jnp.where(
                            ((alignment[block, 0] == lowest + slot) & (live > 0))
                            | ((alignment[block, 1] == lowest + slot) & (live > 1)),
                            1,
                            0,
                        )
                        for slot in range(ALIST)
                    ]
                    start = (lowest - (me * token_blocks - RCH)) * TOKB
                    place = pl.ds(pl.multiple_of(start, 16), span)
                    query = cq[pl.ds(block * BLK, BLK), cols]
                    query = jnp.where(half(query.shape, parity), query, jnp.zeros_like(query))
                    scores = scores_of(query, ck[place, cols]) * scale
                    row = lax.broadcasted_iota(jnp.int32, (span, PAIR), 0)
                    row_ok = jnp.where(row < TOKB, admit[0], admit[1]) > 0
                    value = jnp.where(
                        half((span, PAIR), parity),
                        cv[place, cols],
                        jnp.ones((span, PAIR), jnp.bfloat16),
                    )
                    value = jnp.where(row_ok, value, jnp.zeros_like(value))
                    if shifted:
                        token = lax.broadcasted_iota(jnp.int32, scores.shape, 1)
                        ok = jnp.where(token < TOKB, admit[0], admit[1]) > 0
                        powers = shifted_powers(scores, ok)
                    else:
                        powers = jnp.exp2(scores)
                    acc[parity, pl.ds(block * BLK, BLK), :] = jnp.dot(
                        powers.astype(jnp.bfloat16), value, preferred_element_type=jnp.float32
                    )

            pl.when(safe)(functools.partial(run, False))
            pl.when(jnp.logical_not(safe))(functools.partial(run, True))
        combine(cross_out, cols)
        return carry

    lax.fori_loop(0, MIXED_ATTEND_CNT // 2, cross_pair, 0)
    fetch_wo.wait()
    fetch_wco.wait()

    def finish(index, carry):
        cols = pl.ds(pl.multiple_of(index * CHUNK, CHUNK), CHUNK)
        total = jnp.dot(self_out[...], wo_v[:, cols], preferred_element_type=jnp.float32)
        total += jnp.dot(cross_out[...], wco_v[:, cols], preferred_element_type=jnp.float32)
        out[:, cols] = total.astype(jnp.bfloat16)
        return carry

    lax.fori_loop(0, out.shape[1] // CHUNK, finish, 0)


def shards(
    frames,
    context,
    noise_level,
    alignment,
    counts,
    band_width,
    mod_table,
    qkv_weight,
    out_weight,
    cross_query_weight,
    cross_kv_weight,
    cross_out_weight,
    banded_attender_factor,
    cross_temp,
):
    rows, width = frames.shape
    blocks = rows // BLK
    qw = qkv_weight.shape[1] // 3
    cw = cross_query_weight.shape[1]
    devices = lax.axis_size("seq")
    window_rows = rows + 2 * HALO
    token_rows = context.shape[0] + 2 * RCH * TOKB
    bf16 = jnp.bfloat16
    any_spec = pl.BlockSpec(memory_space=pl.ANY)
    vmem = pl.BlockSpec(memory_space=pltpu.VMEM)
    smem = pl.BlockSpec(memory_space=pltpu.SMEM)
    shapes = [
        (rows, qw),
        (window_rows, qw),
        (window_rows, qw),
        (rows, cw),
        (token_rows, cw),
        (token_rows, cw),
    ]
    projected = pl.pallas_call(
        functools.partial(project_kernel, devices),
        out_shape=[jax.ShapeDtypeStruct(shape, bf16) for shape in shapes],
        in_specs=[any_spec, any_spec, vmem, vmem, any_spec, any_spec, any_spec],
        out_specs=[vmem] * 6,
        scratch_shapes=[
            pltpu.VMEM((window_rows, width), bf16),
            pltpu.VMEM((token_rows, context.shape[1]), bf16),
            pltpu.VMEM((2, 1, blocks), jnp.int32),
            pltpu.VMEM((window_rows, width), bf16),
            pltpu.VMEM(qkv_weight.shape, bf16),
            pltpu.VMEM(cross_query_weight.shape, bf16),
            pltpu.VMEM(cross_kv_weight.shape, bf16),
            pltpu.SemaphoreType.DMA((2,)),
            pltpu.SemaphoreType.DMA((5,)),
            pltpu.SemaphoreType.DMA((2, 3)),
            pltpu.SemaphoreType.DMA((2, 3)),
        ],
        compiler_params=pltpu.CompilerParams(collective_id=0, has_side_effects=True),
        name="project",
    )(
        frames,
        context,
        noise_level.reshape(1, blocks),
        mod_table,
        qkv_weight,
        cross_query_weight,
        cross_kv_weight,
    )
    me = lax.axis_index("seq").astype(jnp.int32).reshape(1)
    return pl.pallas_call(
        functools.partial(attend_kernel, devices),
        out_shape=jax.ShapeDtypeStruct((rows, width), bf16),
        in_specs=[smem] * 6 + [vmem] * 6 + [any_spec] * 2,
        out_specs=vmem,
        scratch_shapes=[
            pltpu.VMEM((2, window_rows, PAIR), bf16),
            pltpu.VMEM((2, rows, PAIR), jnp.float32),
            pltpu.VMEM((rows, qw), bf16),
            pltpu.VMEM((rows, cw), bf16),
            pltpu.VMEM(out_weight.shape, bf16),
            pltpu.VMEM(cross_out_weight.shape, bf16),
            pltpu.SemaphoreType.DMA((2,)),
        ],
        name="attend",
    )(
        me,
        band_width,
        banded_attender_factor,
        cross_temp,
        alignment,
        counts,
        *projected,
        out_weight,
        cross_out_weight,
    )


def solution(mesh):
    placed = (
        P(("groups", "seq"), None),
        P(("groups", "seq"), None),
        P(("groups", "seq")),
        P(("groups", "seq"), None),
        P(("groups", "seq")),
        P(),
        P(),
        P(),
        P(),
        P(),
        P(),
        P(),
        P(),
        P(),
    )
    return jax.shard_map(
        shards, mesh=mesh, in_specs=placed, out_specs=P(("groups", "seq"), None), check_vma=False
    )
```

time: 134 us -> 73.4 us (0.55); the launches traced: 132 us -> 73.2 us
  Pallas kernels: 0 us -> 71.8 us
  matrix products: 53.7 us -> 0 us
  local copies, waits for them, and re-layouts: 40.2 us -> 1.35 us
  other arithmetic: 25.8 us -> 0 us
  starting transfers between devices: 11.5 us -> 0 us
    pallas_call x0 -> x2, Pallas kernels: none -> 71.8 us  [the longest x1 47.6 us: shards(): pl.pallas_call(functools.partial(attend_kernel, devices), out_shape=jax.S...]
    dot_general x9 -> x0, matrix products: 31.9 us -> none  [the longest x1 13.9 us: attend(): jnp.einsum('hij,jhd->ihd', weights, value_rows, preferred_element_type=jn...]
    sub x1 -> x0, matrix products: 21.8 us -> none  [masked_softmax(): powers = jnp.exp(scores - peak)]
    mul x9 -> x0, local copies, waits for them, and re-layouts: 17.8 us -> none  [the longest x6 11 us: head_norm(): parts * lax.rsqrt(jnp.mean(parts * parts, axis=-1, keepdims=True) + 1e-06)]
    slice x7 -> x0, local copies, waits for them, and re-layouts: 15.3 us -> none  [the longest x2 6.37 us: attend(): key_rows = key_pairs[:, :query_width].reshape(-1, BANDED_ATTEND_CT, HD)]
    ppermute x4 -> x0, starting transfers between devices: 11.5 us -> none  [the longest x2 7.46 us: with_halo(): lax.ppermute(lax.slice_in_dim(block, block.shape[dim] - width, None, axis...]
    convert_element_type x3 -> x0, other arithmetic: 7.36 us -> none  [the longest x1 5.25 us: shards(): head_norm(projected[:, :query_width], BANDED_ATTEND_CT).astype(jnp.bfloat16)]
    reduce_sum x4 -> x0, other arithmetic: 6.35 us -> none  [the longest x3 4.85 us: head_norm(): jnp.mean(parts * parts, axis=-1, keepdims=True) + 1e-06]
  transfers between devices with their start and end apart: 4 -> 0, of which waited for: 0 -> 0; matrix products, arithmetic and copies ran while one was open for 51% -> 0% of each run, Pallas kernels for 0% -> 0%
where the time goes in v1:
time: 73.4 us; the launch traced here: 73.2 us
  Pallas kernels  71.8 us (98%)
  local copies, waits for them, and re-layouts  1.35 us (2%)
    pallas_call x1, Pallas kernels, shards(): pl.pallas_call(functools.partial(attend_kernel, devices), out_shape=jax.S...  47.6 us
    pallas_call x1, Pallas kernels, shards(): pl.pallas_call(functools.partial(project_kernel, devices), out_shape=[jax...  24.2 us

profile of v1, /device:TPU:25, one launch (start us, length us, event | category | flops | bytes accessed | tf_op | source)
XLA Modules:
  0.0 73.2 jit_solution(658318456818299844)
XLA Ops:
  0.0 1.4 %copy.15.alignment = s32[4,2]{1,0:T(4,128)} copy(s32[4,2]{0,1:T(2,128)} %param.17) | data formatting | bytes 64 | tf_op args[3]
  1.4 24.2 %project.1 = (bf16[512,1024]{1,0:T(8,128)(2,1)}, bf16[1024,1024]{1,0:T(8,128)(2,1)}, bf16[1024,1024]{1,0:T(8,128)(2,1)}, bf16[512,512]{1,0:T(8,128)(2,1)}, bf16[...) custom-call(bf16[512,1024]{1,0:T(8,128)(2,1)} %frames.1, bf16[96,512]{1,0:T(8,128)(2,1)} %context.1, s32[1,4]{1,0:T(1,128)} %bitcast.2, ...), custom_call_target="tpu_custom_call" | custom-call | tf_op jit(solution)/shard_map/project/pallas_call | solution.py:459
  25.6 47.6 %attend.1 = bf16[512,1024]{1,0:T(8,128)(2,1)} custom-call(s32[1]{0:T(128)} %bitcast.me_ref, s32[16]{0:T(128)} %band.1, f32[16]{0:T(128)} %factor.1, f32[8]{0:T(128)} %temp.1, s32[4,2]{1,0:T(4,128)} %copy.15.alignment, s32[4]{0:T(128)} %counts.1, bf16[512,1024]{1,0:T(8,128)(2,1)} %get-tuple-element.11.q, bf16[1024,1024]{1,0:T(8,128)(2,1)} %get-tuple-element.12.k, ...), custom_call_target="tpu_custom_call" | custom-call | tf_op jit(solution)/shard_map/attend/pallas_call | solution.py:489

commit v2 on v1

v2 whole, which is shorter than its diff:
```python
import functools
import math

import jax
import jax.numpy as jnp
from jax import lax
from jax.experimental import pallas as pl
from jax.experimental.pallas import tpu as pltpu
from jax.sharding import PartitionSpec as P

BANDED_ATTEND_CT = 16
MIXED_ATTEND_CNT = 8
HD = 64
LEVELS = 8
BLK = 128
WMAX = 2
TOKB = 48
RCH = 1
ALIST = 2
PAIR = 2 * HD
HALO = WMAX * BLK
CHUNK = 256
SLAB = 32
EPS = 1e-06
VMEM_LIMIT = 32 * 1024 * 1024
PROJECT_VMEM = 54 * 1024 * 1024
SAFE_FACTOR = 6.0
MESH = pl.DeviceIdType.MESH


def pair_norm(part):
    low = lax.broadcasted_iota(jnp.int32, part.shape, 1) < HD
    square = part * part
    first = jnp.sum(jnp.where(low, square, 0.0), axis=-1, keepdims=True)
    second = jnp.sum(jnp.where(low, 0.0, square), axis=-1, keepdims=True)
    mean = jnp.where(low, first, second) * (1.0 / HD)
    return part * lax.rsqrt(mean + EPS)


def project_kernel(
    devices,
    frames,
    context,
    noise,
    mod,
    wqkv,
    wcq,
    wckv,
    q_out,
    k_out,
    v_out,
    cq_out,
    ck_out,
    cv_out,
    window,
    tokens,
    noise_halo,
    hidden,
    wqkv_v,
    wcq_v,
    wckv_v,
    local_sem,
    weight_sem,
    send_sem,
    recv_sem,
):
    me = lax.axis_index("seq")
    rows, width = frames.shape
    blocks = rows // BLK
    token_rows = context.shape[0]
    margin = RCH * TOKB
    qw = q_out.shape[1]
    cw = cq_out.shape[1]
    has = (me > 0, me < devices - 1)

    fetch_frames = pltpu.make_async_copy(
        frames, window.at[pl.ds(HALO, rows), :], local_sem.at[0]
    )
    fetch_tokens = pltpu.make_async_copy(
        context, tokens.at[pl.ds(margin, token_rows), :], local_sem.at[1]
    )
    fetch_frames.start()
    weight_order = (1, 2, 0)
    fetch_w = {}
    for slot in weight_order:
        cols = pl.ds(slot * qw, qw)
        fetch_w[slot] = pltpu.make_async_copy(
            wqkv.at[:, cols], wqkv_v.at[:, cols], weight_sem.at[slot]
        )
        fetch_w[slot].start()
    fetch_cq = pltpu.make_async_copy(wcq, wcq_v, weight_sem.at[3])
    fetch_ckv = pltpu.make_async_copy(wckv, wckv_v, weight_sem.at[4])

    barrier = pltpu.get_barrier_semaphore()
    for side in (0, 1):

        @pl.when(has[side])
        def _(side=side):
            pl.semaphore_signal(
                barrier, inc=1, device_id={"seq": me + 2 * side - 1}, device_id_type=MESH
            )

    peers = jnp.minimum(me, 1) + jnp.minimum(devices - 1 - me, 1)
    pl.semaphore_wait(barrier, peers)

    def copies(side):
        other = 1 - side
        peer = {"seq": me + 2 * side - 1}
        edge = rows - HALO if side else 0
        land = 0 if side else HALO + rows
        token_edge = token_rows - margin if side else 0
        token_land = 0 if side else margin + token_rows
        triples = (
            (noise, noise_halo.at[other]),
            (frames.at[pl.ds(edge, HALO), :], window.at[pl.ds(land, HALO), :]),
            (
                context.at[pl.ds(token_edge, margin), :],
                tokens.at[pl.ds(token_land, margin), :],
            ),
        )
        return [
            pltpu.make_async_remote_copy(
                src_ref=source,
                dst_ref=target,
                send_sem=send_sem.at[side, index],
                recv_sem=recv_sem.at[other, index],
                device_id=peer,
                device_id_type=MESH,
            )
            for index, (source, target) in enumerate(triples)
        ]

    sends = [copies(0), copies(1)]
    for side in (0, 1):

        @pl.when(has[side])
        def _(side=side):
            for copy in sends[side]:
                copy.start()

    fetch_cq.start()
    fetch_ckv.start()
    fetch_tokens.start()

    def make_hidden(row, level):
        scale = jnp.zeros((1, width), jnp.float32)
        shift = jnp.zeros((1, width), jnp.float32)
        for entry in range(LEVELS):
            here = level == entry
            scale = jnp.where(here, mod[entry : entry + 1, :width], scale)
            shift = jnp.where(here, mod[entry : entry + 1, width:], shift)
        for slab in range(BLK // SLAB):
            place = pl.ds(pl.multiple_of(row + slab * SLAB, SLAB), SLAB)
            values = window[place, :].astype(jnp.float32)
            mean = jnp.mean(values * values, axis=1, keepdims=True)
            normed = values * lax.rsqrt(mean + EPS)
            hidden[place, :] = (normed * (1.0 + scale) + shift).astype(jnp.bfloat16)

    def project(source, place, jobs):
        total = jobs[0][3].shape[1]

        def step(index, carry):
            out_cols = pl.multiple_of(index * CHUNK, CHUNK)
            for target_place, weight, first_col, target, normalize in jobs:
                y = jnp.dot(
                    source[place, :],
                    weight[:, pl.ds(pl.multiple_of(first_col + index * CHUNK, CHUNK), CHUNK)],
                    preferred_element_type=jnp.float32,
                )
                for part in range(CHUNK // PAIR):
                    piece = y[:, part * PAIR : (part + 1) * PAIR]
                    if normalize:
                        piece = pair_norm(piece)
                    target[target_place, pl.ds(out_cols + part * PAIR, PAIR)] = piece.astype(
                        jnp.bfloat16
                    )
            return carry

        lax.fori_loop(0, total // CHUNK, step, 0)

    fetch_frames.wait()
    for block in range(blocks):
        make_hidden(HALO + block * BLK, noise[:, block : block + 1])
    local = pl.ds(HALO, rows)
    for slot in weight_order:
        fetch_w[slot].wait()
    inner = pl.ds(0, rows)
    project(
        hidden,
        local,
        (
            (local, wqkv_v, qw, k_out, True),
            (local, wqkv_v, 2 * qw, v_out, False),
            (inner, wqkv_v, 0, q_out, True),
        ),
    )
    fetch_cq.wait()
    project(hidden, local, ((inner, wcq_v, 0, cq_out, True),))

    fetch_ckv.wait()
    fetch_tokens.wait()

    def halo_step(step, carry):
        side = lax.rem(me + 1 + step, 2)
        present = jnp.where(side == 0, me > 0, me < devices - 1)
        row = pl.multiple_of(side * (HALO + rows), BLK)
        token_row = pl.multiple_of(side * (margin + token_rows), 16)

        @pl.when(present)
        def _():
            waits = (
                noise_halo.at[0],
                window.at[pl.ds(0, HALO), :],
                tokens.at[pl.ds(0, margin), :],
            )
            for index, ref in enumerate(waits):
                pltpu.make_async_copy(ref, ref, recv_sem.at[side, index]).wait()
            levels = noise_halo[side]
            for block in range(WMAX):
                low_side = levels[:, blocks - WMAX + block : blocks - WMAX + block + 1]
                level = jnp.where(side == 0, low_side, levels[:, block : block + 1])
                make_hidden(row + block * BLK, level)

        @pl.when(jnp.logical_not(present))
        def _():
            hidden[pl.ds(row, HALO), :] = jnp.zeros((HALO, width), jnp.bfloat16)
            tokens[pl.ds(token_row, margin), :] = jnp.zeros(
                (margin, tokens.shape[1]), jnp.bfloat16
            )

        place = pl.ds(row, HALO)
        project(
            hidden,
            place,
            ((place, wqkv_v, qw, k_out, True), (place, wqkv_v, 2 * qw, v_out, False)),
        )
        return carry

    lax.fori_loop(0, 2, halo_step, 0)
    every = pl.ds(0, tokens.shape[0])
    project(
        tokens,
        every,
        ((every, wckv_v, 0, ck_out, True), (every, wckv_v, cw, cv_out, False)),
    )

    for side in (0, 1):

        @pl.when(has[side])
        def _(side=side):
            for copy in sends[side]:
                copy.wait_send()


def attend_kernel(
    devices,
    me_ref,
    band,
    factor,
    temp,
    alignment,
    counts,
    q,
    k,
    v,
    cq,
    ck,
    cv,
    wo,
    wco,
    out,
    ones,
    self_out,
    cross_out,
):
    me = me_ref[0]
    rows = q.shape[0]
    blocks = rows // BLK
    window_rows = k.shape[0]
    span = ALIST * TOKB
    to_base2 = HD ** (-0.5) * math.log2(math.e)

    def half(shape, parity):
        lane = lax.broadcasted_iota(jnp.int32, shape, 1)
        return (lane < HD) if parity == 0 else (lane >= HD)

    def scores_of(query, key):
        return lax.dot_general(
            query, key, (((1,), (1,)), ((), ())), preferred_element_type=jnp.float32
        )

    def shifted_powers(scores, allowed):
        scores = jnp.where(allowed, scores, -jnp.inf)
        return jnp.exp2(scores - jnp.max(scores, axis=-1, keepdims=True))

    row_block = (
        lax.broadcasted_iota(jnp.int32, (window_rows, PAIR), 0) // BLK + me * blocks - WMAX
    )
    valid = (row_block >= 0) & (row_block < devices * blocks)
    ones[...] = jnp.where(valid, 1.0, 0.0).astype(jnp.bfloat16)

    def half_query(source, block, cols, parity):
        query = source[pl.ds(block * BLK, BLK), cols]
        return jnp.where(half(query.shape, parity), query, jnp.zeros_like(query))

    def merge(first, second):
        low = half(first.shape, 0)
        total = pltpu.roll(jnp.where(low, second, first), HD, 1)
        return (jnp.where(low, first, second) / total).astype(jnp.bfloat16)

    def self_pair(pair, carry):
        cols = pl.ds(pl.multiple_of(pair * PAIR, PAIR), PAIR)
        reaches = [band[2 * pair + parity] for parity in (0, 1)]
        scales = [factor[2 * pair + parity] * to_base2 for parity in (0, 1)]
        safe = (factor[2 * pair] <= SAFE_FACTOR) & (factor[2 * pair + 1] <= SAFE_FACTOR)

        def fast(sizes):
            for block in range(blocks):
                sums = []
                for parity in (0, 1):
                    size = sizes[parity]
                    keys = pl.ds((block + WMAX - size) * BLK, (2 * size + 1) * BLK)
                    query = half_query(q, block, cols, parity)
                    value = v[keys, cols]
                    value = jnp.where(half(value.shape, parity), value, ones[keys, :])
                    powers = jnp.exp2(scores_of(query, k[keys, cols]) * scales[parity])
                    sums.append(
                        jnp.dot(
                            powers.astype(jnp.bfloat16), value, preferred_element_type=jnp.float32
                        )
                    )
                self_out[pl.ds(block * BLK, BLK), cols] = merge(*sums)

        for low_size in range(WMAX + 1):
            for high_size in range(WMAX + 1):
                pl.when(safe & (reaches[0] == low_size) & (reaches[1] == high_size))(
                    functools.partial(fast, (low_size, high_size))
                )

        @pl.when(jnp.logical_not(safe))
        def _():
            def one(block, inner):
                first = pl.multiple_of(block * BLK, BLK)
                keys = pl.ds(first, (2 * WMAX + 1) * BLK)
                sums = []
                for parity in (0, 1):
                    query = q[pl.ds(first, BLK), cols]
                    query = jnp.where(half(query.shape, parity), query, jnp.zeros_like(query))
                    scores = scores_of(query, k[keys, cols]) * scales[parity]
                    offset = lax.broadcasted_iota(jnp.int32, scores.shape, 1) // BLK - WMAX
                    key_block = offset + block + me * blocks
                    allowed = (
                        (jnp.abs(offset) <= reaches[parity])
                        & (key_block >= 0)
                        & (key_block < devices * blocks)
                    )
                    value = v[keys, cols]
                    value = jnp.where(half(value.shape, parity), value, ones[keys, :])
                    sums.append(
                        jnp.dot(
                            shifted_powers(scores, allowed).astype(jnp.bfloat16),
                            value,
                            preferred_element_type=jnp.float32,
                        )
                    )
                self_out[pl.ds(first, BLK), cols] = merge(*sums)
                return inner

            lax.fori_loop(0, blocks, one, 0)

        return carry

    lax.fori_loop(0, BANDED_ATTEND_CT // 2, self_pair, 0)

    token_blocks = ck.shape[0] // TOKB - 2 * RCH

    def cross_pair(pair, carry):
        cols = pl.ds(pl.multiple_of(pair * PAIR, PAIR), PAIR)
        scales = [temp[2 * pair + parity] * to_base2 for parity in (0, 1)]
        safe = (temp[2 * pair] <= SAFE_FACTOR) & (temp[2 * pair + 1] <= SAFE_FACTOR)

        def run(shifted):
            for block in range(blocks):
                listed = [alignment[slot, block] for slot in range(ALIST)]
                lowest = jnp.minimum(listed[0], listed[1])
                live = counts[block]
                admit = [
                    jnp.where(
                        ((listed[0] == lowest + slot) & (live > 0))
                        | ((listed[1] == lowest + slot) & (live > 1)),
                        1,
                        0,
                    )
                    for slot in range(ALIST)
                ]
                start = (lowest - (me * token_blocks - RCH)) * TOKB
                place = pl.ds(pl.multiple_of(start, 16), span)
                row = lax.broadcasted_iota(jnp.int32, (span, PAIR), 0)
                row_ok = jnp.where(row < TOKB, admit[0], admit[1]) > 0
                sums = []
                for parity in (0, 1):
                    query = half_query(cq, block, cols, parity)
                    scores = scores_of(query, ck[place, cols]) * scales[parity]
                    value = cv[place, cols]
                    value = jnp.where(half(value.shape, parity), value, jnp.ones_like(value))
                    value = jnp.where(row_ok, value, jnp.zeros_like(value))
                    if shifted:
                        token = lax.broadcasted_iota(jnp.int32, scores.shape, 1)
                        ok = jnp.where(token < TOKB, admit[0], admit[1]) > 0
                        powers = shifted_powers(scores, ok)
                    else:
                        powers = jnp.exp2(scores)
                    sums.append(
                        jnp.dot(
                            powers.astype(jnp.bfloat16), value, preferred_element_type=jnp.float32
                        )
                    )
                cross_out[pl.ds(block * BLK, BLK), cols] = merge(*sums)

        pl.when(safe)(functools.partial(run, False))
        pl.when(jnp.logical_not(safe))(functools.partial(run, True))
        return carry

    lax.fori_loop(0, MIXED_ATTEND_CNT // 2, cross_pair, 0)
    def finish(index, carry):
        cols = pl.ds(pl.multiple_of(index * CHUNK, CHUNK), CHUNK)
        total = jnp.dot(self_out[...], wo[:, cols], preferred_element_type=jnp.float32)
        total += jnp.dot(cross_out[...], wco[:, cols], preferred_element_type=jnp.float32)
        out[:, cols] = total.astype(jnp.bfloat16)
        return carry

    lax.fori_loop(0, out.shape[1] // CHUNK, finish, 0)


def shards(
    frames,
    context,
    noise_level,
    alignment,
    counts,
    band_width,
    mod_table,
    qkv_weight,
    out_weight,
    cross_query_weight,
    cross_kv_weight,
    cross_out_weight,
    banded_attender_factor,
    cross_temp,
):
    rows, width = frames.shape
    blocks = rows // BLK
    qw = qkv_weight.shape[1] // 3
    cw = cross_query_weight.shape[1]
    devices = lax.axis_size("seq")
    window_rows = rows + 2 * HALO
    token_rows = context.shape[0] + 2 * RCH * TOKB
    bf16 = jnp.bfloat16
    hbm = pl.BlockSpec(memory_space=pltpu.HBM)
    vmem = pl.BlockSpec(memory_space=pltpu.VMEM)
    smem = pl.BlockSpec(memory_space=pltpu.SMEM)
    shapes = [
        (rows, qw),
        (window_rows, qw),
        (window_rows, qw),
        (rows, cw),
        (token_rows, cw),
        (token_rows, cw),
    ]
    projected = pl.pallas_call(
        functools.partial(project_kernel, devices),
        out_shape=[pltpu.VMEM(shape, bf16) for shape in shapes],
        in_specs=[hbm, hbm, vmem, vmem, hbm, hbm, hbm],
        out_specs=[vmem] * 6,
        scratch_shapes=[
            pltpu.VMEM((window_rows, width), bf16),
            pltpu.VMEM((token_rows, context.shape[1]), bf16),
            pltpu.VMEM((2, 1, blocks), jnp.int32),
            pltpu.VMEM((window_rows, width), bf16),
            pltpu.VMEM(qkv_weight.shape, bf16),
            pltpu.VMEM(cross_query_weight.shape, bf16),
            pltpu.VMEM(cross_kv_weight.shape, bf16),
            pltpu.SemaphoreType.DMA((2,)),
            pltpu.SemaphoreType.DMA((5,)),
            pltpu.SemaphoreType.DMA((2, 3)),
            pltpu.SemaphoreType.DMA((2, 3)),
        ],
        compiler_params=pltpu.CompilerParams(
            collective_id=0, has_side_effects=True, vmem_limit_bytes=PROJECT_VMEM
        ),
        name="project",
    )(
        frames,
        context,
        noise_level.reshape(1, blocks),
        mod_table,
        qkv_weight,
        cross_query_weight,
        cross_kv_weight,
    )
    me = lax.axis_index("seq").astype(jnp.int32).reshape(1)
    return pl.pallas_call(
        functools.partial(attend_kernel, devices),
        out_shape=jax.ShapeDtypeStruct((rows, width), bf16),
        in_specs=[smem] * 6 + [vmem] * 8,
        out_specs=vmem,
        scratch_shapes=[
            pltpu.VMEM((window_rows, PAIR), bf16),
            pltpu.VMEM((rows, qw), bf16),
            pltpu.VMEM((rows, cw), bf16),
        ],
        compiler_params=pltpu.CompilerParams(vmem_limit_bytes=VMEM_LIMIT),
        name="attend",
    )(
        me,
        band_width,
        banded_attender_factor,
        cross_temp,
        alignment.T,
        counts,
        *projected,
        out_weight,
        cross_out_weight,
    )


def solution(mesh):
    placed = (
        P(("groups", "seq"), None),
        P(("groups", "seq"), None),
        P(("groups", "seq")),
        P(("groups", "seq"), None),
        P(("groups", "seq")),
        P(),
        P(),
        P(),
        P(),
        P(),
        P(),
        P(),
        P(),
        P(),
    )
    return jax.shard_map(
        shards, mesh=mesh, in_specs=placed, out_specs=P(("groups", "seq"), None), check_vma=False
    )
```

time: 73.4 us -> 60.3 us (0.82)
  Pallas kernels: 71.8 us -> 60 us
  local copies, waits for them, and re-layouts: 1.35 us -> 0.03 us
    pallas_call x1, Pallas kernels: 47.6 us -> 39.5 us  [shards(): pl.pallas_call(functools.partial(attend_kernel, devices), out_shape=jax.S...]
    pallas_call x1, Pallas kernels: 24.2 us -> 20.5 us  [shards(): pl.pallas_call(functools.partial(project_kernel, devices), out_shape=[plt...]
    unnamed x1 -> x14, local copies, waits for them, and re-layouts: 1.35 us -> 0.03 us
where the time goes in v2:
time: 60.3 us; the launch traced here: 60.1 us
  Pallas kernels  60 us (100%)
    pallas_call x1, Pallas kernels, shards(): pl.pallas_call(functools.partial(attend_kernel, devices), out_shape=jax.S...  39.5 us
    pallas_call x1, Pallas kernels, shards(): pl.pallas_call(functools.partial(project_kernel, devices), out_shape=[plt...  20.5 us

profile of v2, /device:TPU:25, one launch (start us, length us, event | category | flops | bytes accessed | tf_op | source)
XLA Modules:
  0.0 60.1 jit_solution(17743558310886214607)
XLA Ops:
  0.0 0.0 copy-start
  0.0 0.0 copy-start.1
  0.0 0.0 copy-start.2
  0.0 0.0 copy-start.3
  0.0 0.0 copy-start.4
  0.0 0.0 copy-start.5
  0.0 0.0 copy-start.6
  0.0 20.5 %project.1 = (bf16[512,1024]{1,0:T(8,128)(2,1)S(1)}, bf16[1024,1024]{1,0:T(8,128)(2,1)S(1)}, bf16[1024,1024]{1,0:T(8,128)(2,1)S(1)}, bf16[512,512]{1,0:T(8,128)(...) custom-call(bf16[512,1024]{1,0:T(8,128)(2,1)} %frames.1, bf16[96,512]{1,0:T(8,128)(2,1)} %context.1, ...), custom_call_target="tpu_custom_call" | custom-call | tf_op jit(solution)/shard_map/project/pallas_call | solution.py:470
  20.6 0.0 copy-done
  20.6 0.0 copy-done.1
  20.6 0.0 copy-done.2
  20.6 0.0 copy-done.3
  20.6 0.0 copy-done.4
  20.6 0.0 copy-done.5
  20.6 0.0 copy-done.6
  20.6 39.5 %attend.1 = bf16[512,1024]{1,0:T(8,128)(2,1)} custom-call(s32[1]{0:T(128)} %bitcast.me_ref, s32[16]{0:T(128)S(1)} %copy-done.3, f32[16]{0:T(128)S(1)} %copy-done.4, f32[8]{0:T(128)S(1)} %copy-done.5, s32[2,4]{1,0:T(2,128)S(1)} %bitcast.3, s32[4]{0:T(128)S(1)} %copy-done.6, bf16[512,1024]{1,0:T(8,128)(2,1)S(1)} %get-tuple-element.11.q, ...), custom_call_target="tpu_custom_call" | custom-call | tf_op jit(solution)/shard_map/attend/pallas_call | solution.py:502
Async XLA Ops:
  0.0 20.6 %copy-start = (bf16[1024,1024]{1,0:T(8,128)(2,1)S(1)}, bf16[1024,1024]{1,0:T(8,128)(2,1)}, u32[]{:S(2)}) copy-start(bf16[1024,1024]{1,0:T(8,128)(2,1)} %wo.1) | copy-start | bytes 6291460
  0.0 20.6 %copy-start.1 = (bf16[512,1024]{1,0:T(8,128)(2,1)S(1)}, bf16[512,1024]{1,0:T(8,128)(2,1)}, u32[]{:S(2)}) copy-start(bf16[512,1024]{1,0:T(8,128)(2,1)} %wco.1) | copy-start | bytes 3145732
  0.0 20.6 %copy-start.2 = (s32[4,2]{0,1:T(2,128)S(1)}, s32[4,2]{0,1:T(2,128)}, u32[]{:S(2)}) copy-start(s32[4,2]{0,1:T(2,128)} %param.17) | copy-start | bytes 100
  0.0 20.6 %copy-start.3 = (s32[16]{0:T(128)S(1)}, s32[16]{0:T(128)}, u32[]{:S(2)}) copy-start(s32[16]{0:T(128)} %band.1) | copy-start | bytes 196
  0.0 20.6 %copy-start.4 = (f32[16]{0:T(128)S(1)}, f32[16]{0:T(128)}, u32[]{:S(2)}) copy-start(f32[16]{0:T(128)} %factor.1) | copy-start | bytes 196
  0.0 20.6 %copy-start.5 = (f32[8]{0:T(128)S(1)}, f32[8]{0:T(128)}, u32[]{:S(2)}) copy-start(f32[8]{0:T(128)} %temp.1) | copy-start | bytes 100
  0.0 20.6 %copy-start.6 = (s32[4]{0:T(128)S(1)}, s32[4]{0:T(128)}, u32[]{:S(2)}) copy-start(s32[4]{0:T(128)} %counts.1) | copy-start | bytes 52

commit v3 on v2

--- a/solution.py
+++ b/solution.py
@@ -112,11 +112,11 @@
         token_land = 0 if side else margin + token_rows
         triples = (
             (noise, noise_halo.at[other]),
-            (frames.at[pl.ds(edge, HALO), :], window.at[pl.ds(land, HALO), :]),
             (
                 context.at[pl.ds(token_edge, margin), :],
                 tokens.at[pl.ds(token_land, margin), :],
             ),
+            (frames.at[pl.ds(edge, HALO), :], window.at[pl.ds(land, HALO), :]),
         )
         return [
             pltpu.make_async_remote_copy(
@@ -199,21 +199,33 @@
 
     fetch_ckv.wait()
     fetch_tokens.wait()
+    for side in (0, 1):
+        token_place = pl.ds(side * (margin + token_rows), margin)
+
+        @pl.when(has[side])
+        def _(side=side, token_place=token_place):
+            ref = tokens.at[token_place, :]
+            pltpu.make_async_copy(ref, ref, recv_sem.at[side, 1]).wait()
+
+        @pl.when(jnp.logical_not(has[side]))
+        def _(token_place=token_place):
+            tokens[token_place, :] = jnp.zeros((margin, tokens.shape[1]), jnp.bfloat16)
+
+    every = pl.ds(0, tokens.shape[0])
+    project(
+        tokens,
+        every,
+        ((every, wckv_v, 0, ck_out, True), (every, wckv_v, cw, cv_out, False)),
+    )
 
     def halo_step(step, carry):
         side = lax.rem(me + 1 + step, 2)
         present = jnp.where(side == 0, me > 0, me < devices - 1)
         row = pl.multiple_of(side * (HALO + rows), BLK)
-        token_row = pl.multiple_of(side * (margin + token_rows), 16)
 
         @pl.when(present)
         def _():
-            waits = (
-                noise_halo.at[0],
-                window.at[pl.ds(0, HALO), :],
-                tokens.at[pl.ds(0, margin), :],
-            )
-            for index, ref in enumerate(waits):
+            for index, ref in ((0, noise_halo.at[0]), (2, window.at[pl.ds(0, HALO), :])):
                 pltpu.make_async_copy(ref, ref, recv_sem.at[side, index]).wait()
             levels = noise_halo[side]
             for block in range(WMAX):
@@ -224,9 +236,6 @@
         @pl.when(jnp.logical_not(present))
         def _():
             hidden[pl.ds(row, HALO), :] = jnp.zeros((HALO, width), jnp.bfloat16)
-            tokens[pl.ds(token_row, margin), :] = jnp.zeros(
-                (margin, tokens.shape[1]), jnp.bfloat16
-            )
 
         place = pl.ds(row, HALO)
         project(
@@ -237,12 +246,6 @@
         return carry
 
     lax.fori_loop(0, 2, halo_step, 0)
-    every = pl.ds(0, tokens.shape[0])
-    project(
-        tokens,
-        every,
-        ((every, wckv_v, 0, ck_out, True), (every, wckv_v, cw, cv_out, False)),
-    )
 
     for side in (0, 1):
 
@@ -314,16 +317,27 @@
         scales = [factor[2 * pair + parity] * to_base2 for parity in (0, 1)]
         safe = (factor[2 * pair] <= SAFE_FACTOR) & (factor[2 * pair + 1] <= SAFE_FACTOR)
 
+        def tiles(query, block, first, last):
+            keys = pl.ds((block + WMAX + first) * BLK, (last - first) * BLK)
+            return scores_of(query, k[keys, cols])
+
         def fast(sizes):
             for block in range(blocks):
+                queries = [half_query(q, block, cols, parity) for parity in (0, 1)]
+                common = min(sizes)
+                shared = tiles(jnp.concatenate(queries, axis=0), block, -common, common + 1)
                 sums = []
                 for parity in (0, 1):
                     size = sizes[parity]
                     keys = pl.ds((block + WMAX - size) * BLK, (2 * size + 1) * BLK)
-                    query = half_query(q, block, cols, parity)
+                    scores = shared[parity * BLK : (parity + 1) * BLK, :]
+                    if size > common:
+                        left = tiles(queries[parity], block, -size, -common)
+                        right = tiles(queries[parity], block, common + 1, size + 1)
+                        scores = jnp.concatenate([left, scores, right], axis=1)
+                    powers = jnp.exp2(scores * scales[parity])
                     value = v[keys, cols]
                     value = jnp.where(half(value.shape, parity), value, ones[keys, :])
-                    powers = jnp.exp2(scores_of(query, k[keys, cols]) * scales[parity])
                     sums.append(
                         jnp.dot(
                             powers.astype(jnp.bfloat16), value, preferred_element_type=jnp.float32
@@ -397,10 +411,11 @@
                 place = pl.ds(pl.multiple_of(start, 16), span)
                 row = lax.broadcasted_iota(jnp.int32, (span, PAIR), 0)
                 row_ok = jnp.where(row < TOKB, admit[0], admit[1]) > 0
+                queries = [half_query(cq, block, cols, parity) for parity in (0, 1)]
+                both = scores_of(jnp.concatenate(queries, axis=0), ck[place, cols])
                 sums = []
                 for parity in (0, 1):
-                    query = half_query(cq, block, cols, parity)
-                    scores = scores_of(query, ck[place, cols]) * scales[parity]
+                    scores = both[parity * BLK : (parity + 1) * BLK, :] * scales[parity]
                     value = cv[place, cols]
                     value = jnp.where(half(value.shape, parity), value, jnp.ones_like(value))
                     value = jnp.where(row_ok, value, jnp.zeros_like(value))

time: 60.3 us -> 55 us (0.912)
  Pallas kernels: 60 us -> 54.7 us
    pallas_call x1, Pallas kernels: 39.5 us -> 35.1 us  [shards(): pl.pallas_call(functools.partial(attend_kernel, devices), out_shape=jax.S...]
    pallas_call x1, Pallas kernels: 20.5 us -> 19.7 us  [shards(): pl.pallas_call(functools.partial(project_kernel, devices), out_shape=[plt...]
where the time goes in v3:
time: 55 us; the launch traced here: 54.9 us
  Pallas kernels  54.7 us (99%)
    pallas_call x1, Pallas kernels, shards(): pl.pallas_call(functools.partial(attend_kernel, devices), out_shape=jax.S...  35.1 us
    pallas_call x1, Pallas kernels, shards(): pl.pallas_call(functools.partial(project_kernel, devices), out_shape=[plt...  19.7 us

profile of v3, /device:TPU:25, one launch (start us, length us, event | category | flops | bytes accessed | tf_op | source)
XLA Modules:
  0.0 54.9 jit_solution(14445916181527321505)
XLA Ops:
  0.0 0.0 copy-start
  0.0 0.0 copy-start.1
  0.0 0.0 copy-start.2
  0.0 0.0 copy-start.3
  0.0 0.0 copy-start.4
  0.0 0.0 copy-start.5
  0.0 0.0 copy-start.6
  0.0 19.7 %project.1 = (bf16[512,1024]{1,0:T(8,128)(2,1)S(1)}, bf16[1024,1024]{1,0:T(8,128)(2,1)S(1)}, bf16[1024,1024]{1,0:T(8,128)(2,1)S(1)}, bf16[512,512]{1,0:T(8,128)(...) custom-call(bf16[512,1024]{1,0:T(8,128)(2,1)} %frames.1, bf16[96,512]{1,0:T(8,128)(2,1)} %context.1, ...), custom_call_target="tpu_custom_call" | custom-call | tf_op jit(solution)/shard_map/project/pallas_call | solution.py:485
  19.7 0.0 copy-done
  19.7 0.0 copy-done.1
  19.7 0.0 copy-done.2
  19.7 0.0 copy-done.3
  19.7 0.0 copy-done.4
  19.8 0.0 copy-done.5
  19.8 0.0 copy-done.6
  19.8 35.1 %attend.1 = bf16[512,1024]{1,0:T(8,128)(2,1)} custom-call(s32[1]{0:T(128)} %bitcast.me_ref, s32[16]{0:T(128)S(1)} %copy-done.3, f32[16]{0:T(128)S(1)} %copy-done.4, f32[8]{0:T(128)S(1)} %copy-done.5, s32[2,4]{1,0:T(2,128)S(1)} %bitcast.3, s32[4]{0:T(128)S(1)} %copy-done.6, bf16[512,1024]{1,0:T(8,128)(2,1)S(1)} %get-tuple-element.11.q, ...), custom_call_target="tpu_custom_call" | custom-call | tf_op jit(solution)/shard_map/attend/pallas_call | solution.py:517
Async XLA Ops:
  0.0 19.7 %copy-start = (bf16[1024,1024]{1,0:T(8,128)(2,1)S(1)}, bf16[1024,1024]{1,0:T(8,128)(2,1)}, u32[]{:S(2)}) copy-start(bf16[1024,1024]{1,0:T(8,128)(2,1)} %wo.1) | copy-start | bytes 6291460
  0.0 19.7 %copy-start.1 = (bf16[512,1024]{1,0:T(8,128)(2,1)S(1)}, bf16[512,1024]{1,0:T(8,128)(2,1)}, u32[]{:S(2)}) copy-start(bf16[512,1024]{1,0:T(8,128)(2,1)} %wco.1) | copy-start | bytes 3145732
  0.0 19.7 %copy-start.2 = (s32[4,2]{0,1:T(2,128)S(1)}, s32[4,2]{0,1:T(2,128)}, u32[]{:S(2)}) copy-start(s32[4,2]{0,1:T(2,128)} %param.17) | copy-start | bytes 100
  0.0 19.7 %copy-start.3 = (s32[16]{0:T(128)S(1)}, s32[16]{0:T(128)}, u32[]{:S(2)}) copy-start(s32[16]{0:T(128)} %band.1) | copy-start | bytes 196
  0.0 19.7 %copy-start.4 = (f32[16]{0:T(128)S(1)}, f32[16]{0:T(128)}, u32[]{:S(2)}) copy-start(f32[16]{0:T(128)} %factor.1) | copy-start | bytes 196
  0.0 19.7 %copy-start.5 = (f32[8]{0:T(128)S(1)}, f32[8]{0:T(128)}, u32[]{:S(2)}) copy-start(f32[8]{0:T(128)} %temp.1) | copy-start | bytes 100
  0.0 19.7 %copy-start.6 = (s32[4]{0:T(128)S(1)}, s32[4]{0:T(128)}, u32[]{:S(2)}) copy-start(s32[4]{0:T(128)} %counts.1) | copy-start | bytes 52
